TPU v7x, 32 devices: a whole 2x2x4 slice. The times are simulated.
32 devices in a mesh: groups: 2 (over y), frame: 4 (over z), quarter: 2 (over x), sub: 2 (over core).
Axes of the slice: x: 2, y: 2, z: 4, core: 2. Of those that a mesh axis runs over, the one named last changes fastest.
Arguments:
- queries: bfloat16 [16, 1024, 256], P(('groups', 'frame'), ('quarter', 'sub')), parts along dimension 0, may hold values from -36 to 36
- keys: bfloat16 [16, 1024, 256], P(('groups', 'frame'), ('quarter', 'sub')), parts along dimension 0, may hold values from -6 to 6
- values: bfloat16 [16, 1024, 256], P(('groups', 'frame'), ('quarter', 'sub')), parts along dimension 0, may hold values from -6 to 6
Outputs:
- attended: bfloat16 [16, 1024, 256], P(('groups', 'frame'), ('quarter', 'sub')), parts along dimension 0
There are 2 independent parts, one for each index of `groups`. A program takes and returns all parts, laid end to end along the dimension named above; each array names one. Nothing has to cross between parts.
All inputs are finite; a program needn't handle non-finite values.
Results may differ from a plain program's by a relative error of at most 0.0028.
Values may be sent and summed in bfloat16 or wider, within the bound.
A program may use at most 64 MiB of HBM per device.

v0:
```python
import math
import jax
import jax.numpy as jnp
from jax import lax
from jax.sharding import PartitionSpec as P

STRIP = 16


def partial_attend(query_rows, key_rows, value_rows, running, score_scale):
    top_run, sum_run, acc_run = running
    scores = (
        jnp.einsum("frd,fnd->frn", query_rows, key_rows, preferred_element_type=jnp.float32)
        * score_scale
    )
    highest = jnp.maximum(top_run, jnp.max(scores, axis=-1, keepdims=True))
    expo = jnp.exp(scores - highest)
    factor = jnp.exp(top_run - highest)
    sum_next = sum_run * factor + jnp.sum(expo, axis=-1, keepdims=True)
    acc_next = acc_run * factor + jnp.einsum(
        "frn,fnd->frd", expo.astype(jnp.bfloat16), value_rows, preferred_element_type=jnp.float32
    )
    return (highest, sum_next, acc_next)


def fold_keys(query_rows, score_scale, running, pieces):
    key_piece, value_piece = pieces
    length = key_piece.shape[1]
    block_keys = math.gcd(length, 2048)
    for block_index in range(length // block_keys):
        lower = block_index * block_keys
        running = partial_attend(
            query_rows,
            key_piece[:, lower : lower + block_keys],
            value_piece[:, lower : lower + block_keys],
            running,
            score_scale,
        )
    return running


def empty_state(query_rows):
    frames_here, rows_here, width = query_rows.shape
    return (
        jnp.full((frames_here, rows_here, 1), -jnp.inf, jnp.float32),
        jnp.zeros((frames_here, rows_here, 1), jnp.float32),
        jnp.zeros((frames_here, rows_here, width), jnp.float32),
    )


def body(queries, keys, values):
    head_width = queries.shape[2] // 2
    frames_dev = queries.shape[0]
    tokens_dev = queries.shape[1]
    score_scale = 1.0 / math.sqrt(head_width)
    query_spatial = queries[:, :, :head_width]
    key_spatial = keys[:, :, :head_width]
    value_spatial = values[:, :, :head_width]
    frame_count = lax.axis_size("frame")
    local_strips = tokens_dev // (STRIP * frame_count)

    def to_strips(array):
        part_two = array[:, :, head_width:].reshape(
            frames_dev, frame_count, local_strips, STRIP, head_width
        )
        return part_two.transpose(1, 2, 0, 3, 4)

    query_strip = lax.all_to_all(
        to_strips(queries), "frame", split_axis=0, concat_axis=2, tiled=True
    )
    key_strip = lax.all_to_all(to_strips(keys), "frame", split_axis=0, concat_axis=2, tiled=True)
    value_strip = lax.all_to_all(
        to_strips(values), "frame", split_axis=0, concat_axis=2, tiled=True
    )
    item_count = query_strip.shape[1]
    frames_all = query_strip.shape[2]
    rows_strip = frames_all * STRIP
    query_flat = query_strip.reshape(item_count, rows_strip, head_width)
    key_flat = key_strip.reshape(item_count, rows_strip, head_width)
    value_flat = value_strip.reshape(item_count, rows_strip, head_width)
    scores = (
        jnp.einsum("nqd,nkd->nqk", query_flat, key_flat, preferred_element_type=jnp.float32)
        * score_scale
    )
    highest = jnp.max(scores, axis=-1, keepdims=True)
    expo = jnp.exp(scores - highest)
    totals = jnp.sum(expo, axis=-1, keepdims=True)
    mixed = jnp.einsum(
        "nqk,nkd->nqd", expo.astype(jnp.bfloat16), value_flat, preferred_element_type=jnp.float32
    )
    strip_out = (
        (mixed / totals).astype(jnp.bfloat16).reshape(1, item_count, frames_all, STRIP, head_width)
    )
    returned = lax.all_to_all(strip_out, "frame", split_axis=2, concat_axis=0, tiled=True)
    temporal = returned.transpose(2, 0, 1, 3, 4).reshape(frames_dev, tokens_dev, head_width)
    top_all, total_spatial, acc_spatial = fold_keys(
        query_spatial,
        score_scale,
        empty_state(query_spatial),
        (
            lax.all_gather(key_spatial, ("quarter", "sub"), axis=1, tiled=True),
            lax.all_gather(value_spatial, ("quarter", "sub"), axis=1, tiled=True),
        ),
    )
    spatial = (acc_spatial / total_spatial).astype(jnp.bfloat16)
    return jnp.concatenate([spatial, temporal], axis=-1)


def solution(mesh):
    in_specs = (
        P(("groups", "frame"), ("quarter", "sub"), None),
        P(("groups", "frame"), ("quarter", "sub"), None),
        P(("groups", "frame"), ("quarter", "sub"), None),
    )
    out_specs = P(("groups", "frame"), ("quarter", "sub"), None)
    return jax.shard_map(body, mesh=mesh, in_specs=in_specs, out_specs=out_specs, check_vma=False)
```

profile of v0, /device:TPU:0, one launch (start us, length us, event | category | flops | bytes accessed | tf_op | source)
XLA Modules:
  0.0 53.8 jit_solution(1499810248122373728)
XLA Ops:
  0.0 1.0 %fusion.16 = (bf16[2,256,128]{2,1,0:T(8,128)(2,1)S(1)}, bf16[2,256,128]{2,1,0:T(8,128)(2,1)S(1)}) fusion(bf16[2,256,256]{2,1,0:T(8,128)(2,1)} %param.4), kind=kLoop, calls=%fused_computation.22 | loop fusion | bytes 524288 | tf_op jit(solution)/shard_map/slice | solution.py:57
  1.0 0.0 copy-start
  1.0 0.7 %copy.31 = bf16[4,4,2,16,128]{4,3,2,1,0:T(8,128)(2,1)} copy(bf16[4,4,2,16,128]{4,3,1,0,2:T(8,128)(2,1)S(1)} %bitcast.42) | data formatting | bytes 262144 | tf_op jit(solution)/shard_map/transpose | solution.py:66
  1.7 6.3 %all-to-all-start.1 = ((bf16[4,4,2,16,128]{4,3,2,1,0:T(8,128)(2,1)}), bf16[4,4,2,16,128]{4,3,2,1,0:T(8,128)(2,1)S(1)}, u32[]{:S(2)}, u32[]{:S(2)}) async-start(bf16[4,4,2,16,128]{4,3,2,1,0:T(8,128)(2,1)} %copy.31), calls=%async_computation.1 | async-start | bytes 262144 | tf_op jit(solution)/shard_map/all_to_all | solution.py:71
  8.0 0.0 slice-start
  8.0 7.3 %all_gather.6 = bf16[2,1024,128]{2,1,0:T(8,128)(2,1)S(1)} all-gather(bf16[2,256,128]{2,1,0:T(8,128)(2,1)S(1)} %get-tuple-element.5), channel_id=1, replica_groups=mesh['groups'=2,'frame'=4,'quarter'=2,'sub'=2] {'quarter','sub'}, dimensions={1}, use_global_device_ids=true | all-gather | bytes 655360 | tf_op jit(solution)/shard_map/all_gather | solution.py:101
  15.3 1.4 %multiply_reduce_fusion = (f32[2,256]{1,0:T(2,128)S(1)}, f32[2,256,1024]{2,1,0:T(8,128)S(1)}) fusion(bf16[2,1024,128]{2,1,0:T(8,128)(2,1)S(1)} %all_gather.6, bf16[2,256,256]{2,1,0:T(8,128)(2,1)} %param.3), kind=kOutput, calls=%fused_computation.1 | convolution fusion | flops 135265792 | bytes 2754560 | tf_op jit(solution)/shard_map/frd,fnd->frn/dot_general | solution.py:13
  16.7 0.0 copy-done
  16.8 0.1 copy.43
  16.9 0.0 slice-done
  16.9 0.7 %copy.29 = bf16[4,4,2,16,128]{4,3,2,1,0:T(8,128)(2,1)} copy(bf16[4,4,2,16,128]{4,3,1,0,2:T(8,128)(2,1)S(1)} %bitcast.37) | data formatting | bytes 262144 | tf_op jit(solution)/shard_map/transpose | solution.py:66
  17.6 0.7 %copy.33 = bf16[4,4,2,16,128]{4,3,2,1,0:T(8,128)(2,1)} copy(bf16[4,4,2,16,128]{4,3,1,0,2:T(8,128)(2,1)S(1)} %bitcast.41) | data formatting | bytes 262144 | tf_op jit(solution)/shard_map/transpose | solution.py:66
  18.2 0.5 fusion
  18.7 0.0 all-to-all-done.1
  18.7 5.1 %all-to-all-start = ((bf16[4,4,2,16,128]{4,3,2,1,0:T(8,128)(2,1)}), bf16[4,4,2,16,128]{4,3,2,1,0:T(8,128)(2,1)S(1)}, u32[]{:S(2)}, u32[]{:S(2)}) async-start(bf16[4,4,2,16,128]{4,3,2,1,0:T(8,128)(2,1)} %copy.29), calls=%async_computation | async-start | bytes 262144 | tf_op jit(solution)/shard_map/all_to_all | solution.py:68
  23.9 6.4 %all-to-all-done = bf16[4,4,2,16,128]{4,3,2,1,0:T(8,128)(2,1)S(1)} async-done(((bf16[4,4,2,16,128]{4,3,2,1,0:T(8,128)(2,1)}), bf16[4,4,2,16,128]{4,3,2,1,0:T(8,128)(2,1)S(1)}, u32[]{:S(2)}, u32[]{:S(2)}) %all-to-all-start) | async-done | bytes 131104 | tf_op jit(solution)/shard_map/all_to_all | solution.py:68
  30.3 3.3 %all-to-all-start.2 = ((bf16[4,4,2,16,128]{4,3,2,1,0:T(8,128)(2,1)}), bf16[4,4,2,16,128]{4,3,2,1,0:T(8,128)(2,1)S(1)}, u32[]{:S(2)}, u32[]{:S(2)}) async-start(bf16[4,4,2,16,128]{4,3,2,1,0:T(8,128)(2,1)} %copy.33), calls=%async_computation.2 | async-start | bytes 262144 | tf_op jit(solution)/shard_map/all_to_all | solution.py:72
  33.6 6.5 %all_gather.7 = bf16[2,1024,128]{1,2,0:T(8,128)(2,1)S(1)} all-gather(bf16[2,256,128]{1,2,0:T(8,128)(2,1)S(1)} %copy.43), channel_id=1, replica_groups=mesh['groups'=2,'frame'=4,'quarter'=2,'sub'=2] {'quarter','sub'}, dimensions={1}, use_global_device_ids=true | all-gather | bytes 655360 | tf_op jit(solution)/shard_map/all_gather | solution.py:102
  40.1 0.0 all-to-all-done.2
  40.2 0.2 fusion.18
  40.4 0.1 fusion.8
  40.5 0.3 fusion.3
  40.7 0.7 %copy.36 = bf16[1,4,8,16,128]{4,3,1,0,2:T(8,128)(2,1)} copy(bf16[1,4,8,16,128]{4,3,2,1,0:T(8,128)(2,1)S(1)} %bitcast.44) | data formatting | bytes 262144 | tf_op jit(solution)/shard_map/reshape | solution.py:92
  41.4 5.0 %all-to-all-start.3 = ((bf16[1,4,8,16,128]{4,3,1,0,2:T(8,128)(2,1)}), bf16[1,4,8,16,128]{4,3,1,0,2:T(8,128)(2,1)S(1)}, u32[]{:S(2)}, u32[]{:S(2)}) async-start(bf16[1,4,8,16,128]{4,3,1,0,2:T(8,128)(2,1)} %copy.36), calls=%async_computation.3 | async-start | bytes 262144 | tf_op jit(solution)/shard_map/all_to_all | solution.py:94
  46.4 0.6 %fusion.4 = bf16[2,256,128]{1,2,0:T(8,128)(2,1)S(1)} fusion(bf16[2,1024,128]{1,2,0:T(8,128)(2,1)S(1)} %all_gather.7, f32[2,256,1024]{2,1,0:T(8,128)S(1)} %get-tuple-element.14, f32[2,256]{1,0:T(2,128)S(1)} %get-tuple-element.13, f32[2,256]{1,0:T(2,128)S(1)} %get-tuple-element.10, f32[2,256]{1,0:T(2,128)S(1)} %get-tuple-element.9), kind=kOutput, calls=%fused_computation.9 | convolution fusion | flops 135987200 | bytes 2758656 | tf_op jit(solution)/shard_map/frn,fnd->frd/dot_general | solution.py:20
  47.0 5.8 %all-to-all-done.3 = bf16[1,4,8,16,128]{4,3,1,0,2:T(8,128)(2,1)S(1)} async-done(((bf16[1,4,8,16,128]{4,3,1,0,2:T(8,128)(2,1)}), bf16[1,4,8,16,128]{4,3,1,0,2:T(8,128)(2,1)S(1)}, u32[]{:S(2)}, u32[]{:S(2)}) %all-to-all-start.3) | async-done | bytes 131104 | tf_op jit(solution)/shard_map/all_to_all | solution.py:94
  52.9 0.1 copy.39
  53.0 0.8 %copy.40 = bf16[2,256,256]{2,1,0:T(8,128)(2,1)} copy(bf16[2,256,256]{1,2,0:T(8,128)(2,1)S(1)} %pad_maximum_fusion) | data formatting | bytes 524288 | tf_op jit(solution)/shard_map/concatenate | solution.py:106
  (7 shorter events, 0.1 us)
Async XLA Ops:
  1.0 15.7 %copy-start = (bf16[2,256,256]{2,1,0:T(8,128)(2,1)S(1)}, bf16[2,256,256]{2,1,0:T(8,128)(2,1)}, u32[]{:S(2)}) copy-start(bf16[2,256,256]{2,1,0:T(8,128)(2,1)} %param.5) | copy-start | bytes 786436
  1.7 17.1 %all-to-all-start.1 = ((bf16[4,4,2,16,128]{4,3,2,1,0:T(8,128)(2,1)}), bf16[4,4,2,16,128]{4,3,2,1,0:T(8,128)(2,1)S(1)}, u32[]{:S(2)}, u32[]{:S(2)}) async-start(bf16[4,4,2,16,128]{4,3,2,1,0:T(8,128)(2,1)} %copy.31), calls=%async_computation.1 | async-start | bytes 262144 | tf_op jit(solution)/shard_map/all_to_all | solution.py:71
  8.0 8.9 %slice-start = ((bf16[2,256,256]{2,1,0:T(8,128)(2,1)}), bf16[2,256,128]{2,1,0:T(8,128)(2,1)S(1)}, s32[]{:S(2)}) async-start(bf16[2,256,256]{2,1,0:T(8,128)(2,1)} %param.3), calls=%async_computation.4 | async-start | bytes 262144 | tf_op jit(solution)/shard_map/slice | solution.py:63
  18.7 11.5 %all-to-all-start = ((bf16[4,4,2,16,128]{4,3,2,1,0:T(8,128)(2,1)}), bf16[4,4,2,16,128]{4,3,2,1,0:T(8,128)(2,1)S(1)}, u32[]{:S(2)}, u32[]{:S(2)}) async-start(bf16[4,4,2,16,128]{4,3,2,1,0:T(8,128)(2,1)} %copy.29), calls=%async_computation | async-start | bytes 262144 | tf_op jit(solution)/shard_map/all_to_all | solution.py:68
  30.3 9.9 %all-to-all-start.2 = ((bf16[4,4,2,16,128]{4,3,2,1,0:T(8,128)(2,1)}), bf16[4,4,2,16,128]{4,3,2,1,0:T(8,128)(2,1)S(1)}, u32[]{:S(2)}, u32[]{:S(2)}) async-start(bf16[4,4,2,16,128]{4,3,2,1,0:T(8,128)(2,1)} %copy.33), calls=%async_computation.2 | async-start | bytes 262144 | tf_op jit(solution)/shard_map/all_to_all | solution.py:72
  41.4 11.5 %all-to-all-start.3 = ((bf16[1,4,8,16,128]{4,3,1,0,2:T(8,128)(2,1)}), bf16[1,4,8,16,128]{4,3,1,0,2:T(8,128)(2,1)S(1)}, u32[]{:S(2)}, u32[]{:S(2)}) async-start(bf16[1,4,8,16,128]{4,3,1,0,2:T(8,128)(2,1)} %copy.36), calls=%async_computation.3 | async-start | bytes 262144 | tf_op jit(solution)/shard_map/all_to_all | solution.py:94
where the time goes:
time: 54.4 us; the launch traced here: 53.8 us
  starting transfers between devices  19.8 us (36%)
  blocking collectives  13.8 us (25%)
  waiting for transfers between devices  12.2 us (22%)
  local copies, waits for them, and re-layouts  4.8 us (9%)
  matrix products  2.5 us (5%)
  other arithmetic  0.58 us (1%)
    all_gather x1, blocking collectives, body(): lax.all_gather(key_spatial, ('quarter', 'sub'), axis=1, tiled=True)  7.29 us
    all_gather x1, blocking collectives, body(): lax.all_gather(value_spatial, ('quarter', 'sub'), axis=1, tiled=True)  6.5 us
    all_to_all x1, waiting for transfers between devices, body(): lax.all_to_all(to_strips(queries), 'frame', split_axis=0, concat_axis=2,...  6.41 us
    all_to_all x1, starting transfers between devices, body(): lax.all_to_all(to_strips(keys), 'frame', split_axis=0, concat_axis=2, til...  6.35 us
    all_to_all x1, waiting for transfers between devices, body(): lax.all_to_all(strip_out, 'frame', split_axis=2, concat_axis=0, tiled=True)  5.8 us
    all_to_all x1, starting transfers between devices, body(): lax.all_to_all(to_strips(queries), 'frame', split_axis=0, concat_axis=2,...  5.1 us
    all_to_all x1, starting transfers between devices, body(): lax.all_to_all(strip_out, 'frame', split_axis=2, concat_axis=0, tiled=True)  5.04 us
    all_to_all x1, starting transfers between devices, body(): lax.all_to_all(to_strips(values), 'frame', split_axis=0, concat_axis=2, t...  3.33 us
  transfers between devices with their start and end apart: 4, of which 2 were waited for; matrix products, arithmetic and copies ran while one was open for 7% of the time, Pallas kernels for 0%

commit v1 on v0

--- a/solution.py
+++ b/solution.py
@@ -5,6 +5,18 @@
 from jax.sharding import PartitionSpec as P
 
 STRIP = 16
+
+
+def gather_around(array, axis, dim):
+    ways, here, step = (lax.axis_size(axis), lax.axis_index(axis), array.shape[dim])
+    dims = [n * ways if d == dim else n for d, n in enumerate(array.shape)]
+    full = lax.dynamic_update_slice_in_dim(
+        jnp.zeros(dims, array.dtype), array, here * step, axis=dim
+    )
+    for far in range(1, ways):
+        array = lax.ppermute(array, axis, [(d, (d + 1) % ways) for d in range(ways)])
+        full = lax.dynamic_update_slice_in_dim(full, array, (here - far) % ways * step, axis=dim)
+    return full
 
 
 def partial_attend(query_rows, key_rows, value_rows, running, score_scale):
@@ -98,7 +110,7 @@
         score_scale,
         empty_state(query_spatial),
         (
-            lax.all_gather(key_spatial, ("quarter", "sub"), axis=1, tiled=True),
+            gather_around(key_spatial, ("quarter", "sub"), 1),
             lax.all_gather(value_spatial, ("quarter", "sub"), axis=1, tiled=True),
         ),
     )

time: 54.4 us -> 49.9 us (0.917)
  blocking collectives: 13.8 us -> 7.17 us
  waiting for transfers between devices: 12.2 us -> 15.6 us
  starting transfers between devices: 19.8 us -> 18.6 us
  local copies, waits for them, and re-layouts: 4.8 us -> 5.93 us
  matrix products: 2.5 us -> 1.43 us
    all_gather x1 -> x0, blocking collectives: 7.29 us -> none  [body(): lax.all_gather(key_spatial, ('quarter', 'sub'), axis=1, tiled=True)]
    all_to_all x1, waiting for transfers between devices: 0.01 us -> 6.22 us  [body(): lax.all_to_all(to_strips(values), 'frame', split_axis=0, concat_axis=2, t...]
    all_to_all x1, starting transfers between devices: 6.35 us -> 3.32 us  [body(): lax.all_to_all(to_strips(keys), 'frame', split_axis=0, concat_axis=2, til...]
    all_to_all x1, waiting for transfers between devices: 6.41 us -> 4.07 us  [body(): lax.all_to_all(to_strips(queries), 'frame', split_axis=0, concat_axis=2,...]
    all_to_all x1, starting transfers between devices: 3.33 us -> 5.19 us  [body(): lax.all_to_all(to_strips(values), 'frame', split_axis=0, concat_axis=2, t...]
    all_to_all x1, starting transfers between devices: 5.04 us -> 3.33 us  [body(): lax.all_to_all(strip_out, 'frame', split_axis=2, concat_axis=0, tiled=True)]
    all_to_all x1, starting transfers between devices: 5.1 us -> 6.35 us  [body(): lax.all_to_all(to_strips(queries), 'frame', split_axis=0, concat_axis=2,...]
    dot_general x1, matrix products: 1.42 us -> 0.45 us  [partial_attend(): jnp.einsum('frd,fnd->frn', query_rows, key_rows, preferred_element_type=j...]
  transfers between devices with their start and end apart: 4 -> 7, of which waited for: 2 -> 4; matrix products, arithmetic and copies ran while one was open for 7% -> 11% of each run, Pallas kernels for 0% -> 0%
where the time goes in v1:
time: 49.9 us; the launch traced here: 49.4 us
  starting transfers between devices  18.6 us (37%)
  waiting for transfers between devices  15.6 us (31%)
  blocking collectives  7.17 us (14%)
  local copies, waits for them, and re-layouts  5.93 us (12%)
  matrix products  1.43 us (3%)
    all_gather x1, blocking collectives, body(): lax.all_gather(value_spatial, ('quarter', 'sub'), axis=1, tiled=True)  7.17 us
    all_to_all x1, starting transfers between devices, body(): lax.all_to_all(to_strips(queries), 'frame', split_axis=0, concat_axis=2,...  6.35 us
    all_to_all x1, waiting for transfers between devices, body(): lax.all_to_all(to_strips(values), 'frame', split_axis=0, concat_axis=2, t...  6.22 us
    all_to_all x1, starting transfers between devices, body(): lax.all_to_all(to_strips(values), 'frame', split_axis=0, concat_axis=2, t...  5.19 us
    all_to_all x1, waiting for transfers between devices, body(): lax.all_to_all(strip_out, 'frame', split_axis=2, concat_axis=0, tiled=True)  5.18 us
    all_to_all x1, waiting for transfers between devices, body(): lax.all_to_all(to_strips(queries), 'frame', split_axis=0, concat_axis=2,...  4.07 us
    all_to_all x1, starting transfers between devices, body(): lax.all_to_all(strip_out, 'frame', split_axis=2, concat_axis=0, tiled=True)  3.33 us
    all_to_all x1, starting transfers between devices, body(): lax.all_to_all(to_strips(keys), 'frame', split_axis=0, concat_axis=2, til...  3.32 us
  transfers between devices with their start and end apart: 7, of which 4 were waited for; matrix products, arithmetic and copies ran while one was open for 11% of the time, Pallas kernels for 0%

profile of v1, /device:TPU:0, one launch (start us, length us, event | category | flops | bytes accessed | tf_op | source)
XLA Modules:
  0.0 49.4 jit_solution(13055516411273821163)
XLA Ops:
  0.0 0.0 copy-start.1
  0.0 1.0 %slice.21 = bf16[2,256,128]{2,1,0:T(8,128)(2,1)S(1)} slice(bf16[2,256,256]{2,1,0:T(8,128)(2,1)} %param.3), slice={[0:2], [0:256], [128:256]} | slice | bytes 262144 | tf_op jit(solution)/shard_map/slice | solution.py:75
  1.0 0.7 %copy.33 = bf16[4,4,2,16,128]{4,3,2,1,0:T(8,128)(2,1)} copy(bf16[4,4,2,16,128]{4,3,1,0,2:T(8,128)(2,1)S(1)} %bitcast.50) | data formatting | bytes 262144 | tf_op jit(solution)/shard_map/transpose | solution.py:78
  1.6 6.3 %all-to-all-start = ((bf16[4,4,2,16,128]{4,3,2,1,0:T(8,128)(2,1)}), bf16[4,4,2,16,128]{4,3,2,1,0:T(8,128)(2,1)S(1)}, u32[]{:S(2)}, u32[]{:S(2)}) async-start(bf16[4,4,2,16,128]{4,3,2,1,0:T(8,128)(2,1)} %copy.33), calls=%async_computation | async-start | bytes 262144 | tf_op jit(solution)/shard_map/all_to_all | solution.py:80
  8.0 0.1 broadcast_in_dim.7
  8.0 1.0 %fusion.18 = (bf16[2,256,128]{2,1,0:T(8,128)(2,1)S(1)}, bf16[2,1024,128]{2,1,0:T(8,128)(2,1)S(1)}, bf16[2,256,128]{2,1,0:T(8,128)(2,1)S(1)}) fusion(bf16[2,256,256]{2,1,0:T(8,128)(2,1)} %param.4, bf16[2,1024,128]{2,1,0:T(8,128)(2,1)S(1)} %broadcast_in_dim.7, s32[]{:T(128)S(6)} %select_n.27), kind=kLoop, calls=%fused_computation.27 | loop fusion | bytes 655364 | tf_op jit(solution)/shard_map/slice | solution.py:69
  9.1 0.1 collective-permute-start
  9.1 0.7 %copy.35 = bf16[4,4,2,16,128]{4,3,2,1,0:T(8,128)(2,1)} copy(bf16[4,4,2,16,128]{4,3,1,0,2:T(8,128)(2,1)S(1)} %bitcast.53) | data formatting | bytes 262144 | tf_op jit(solution)/shard_map/transpose | solution.py:78
  9.8 0.0 copy-done.1
  9.9 0.1 copy.48
  10.0 4.1 %all-to-all-done = bf16[4,4,2,16,128]{4,3,2,1,0:T(8,128)(2,1)S(1)} async-done(((bf16[4,4,2,16,128]{4,3,2,1,0:T(8,128)(2,1)}), bf16[4,4,2,16,128]{4,3,2,1,0:T(8,128)(2,1)S(1)}, u32[]{:S(2)}, u32[]{:S(2)}) %all-to-all-start) | async-done | bytes 131104 | tf_op jit(solution)/shard_map/all_to_all | solution.py:80
  14.0 3.3 %all-to-all-start.1 = ((bf16[4,4,2,16,128]{4,3,2,1,0:T(8,128)(2,1)}), bf16[4,4,2,16,128]{4,3,2,1,0:T(8,128)(2,1)S(1)}, u32[]{:S(2)}, u32[]{:S(2)}) async-start(bf16[4,4,2,16,128]{4,3,2,1,0:T(8,128)(2,1)} %copy.35), calls=%async_computation.1 | async-start | bytes 262144 | tf_op jit(solution)/shard_map/all_to_all | solution.py:83
  17.4 7.2 %all_gather.3 = bf16[2,1024,128]{1,2,0:T(8,128)(2,1)S(1)} all-gather(bf16[2,256,128]{1,2,0:T(8,128)(2,1)S(1)} %copy.48), channel_id=1, replica_groups=mesh['groups'=2,'frame'=4,'quarter'=2,'sub'=2] {'quarter','sub'}, dimensions={1}, use_global_device_ids=true | all-gather | bytes 655360 | tf_op jit(solution)/shard_map/all_gather | solution.py:114
  24.6 0.7 %copy.37 = bf16[4,4,2,16,128]{4,3,2,1,0:T(8,128)(2,1)} copy(bf16[4,4,2,16,128]{4,3,1,0,2:T(8,128)(2,1)S(1)} %bitcast.51) | data formatting | bytes 262144 | tf_op jit(solution)/shard_map/transpose | solution.py:78
  25.2 0.0 collective-permute-done
  25.2 0.3 collective-permute-start.1
  25.6 0.0 copy-start
  25.6 0.0 all-to-all-done.1
  25.6 5.2 %all-to-all-start.2 = ((bf16[4,4,2,16,128]{4,3,2,1,0:T(8,128)(2,1)}), bf16[4,4,2,16,128]{4,3,2,1,0:T(8,128)(2,1)S(1)}, u32[]{:S(2)}, u32[]{:S(2)}) async-start(bf16[4,4,2,16,128]{4,3,2,1,0:T(8,128)(2,1)} %copy.37), calls=%async_computation.2 | async-start | bytes 262144 | tf_op jit(solution)/shard_map/all_to_all | solution.py:84
  30.8 0.2 fusion.19
  31.0 6.2 %all-to-all-done.2 = bf16[4,4,2,16,128]{4,3,2,1,0:T(8,128)(2,1)S(1)} async-done(((bf16[4,4,2,16,128]{4,3,2,1,0:T(8,128)(2,1)}), bf16[4,4,2,16,128]{4,3,2,1,0:T(8,128)(2,1)S(1)}, u32[]{:S(2)}, u32[]{:S(2)}) %all-to-all-start.2) | async-done | bytes 131104 | tf_op jit(solution)/shard_map/all_to_all | solution.py:84
  37.3 0.1 fusion.7
  37.3 0.0 collective-permute-done.1
  37.4 0.1 collective-permute-start.2
  37.4 0.2 fusion.3
  37.7 0.7 %copy.40 = bf16[1,4,8,16,128]{4,3,1,0,2:T(8,128)(2,1)} copy(bf16[1,4,8,16,128]{4,3,2,1,0:T(8,128)(2,1)S(1)} %bitcast.56) | data formatting | bytes 262144 | tf_op jit(solution)/shard_map/reshape | solution.py:104
  38.3 3.3 %all-to-all-start.3 = ((bf16[1,4,8,16,128]{4,3,1,0,2:T(8,128)(2,1)}), bf16[1,4,8,16,128]{4,3,1,0,2:T(8,128)(2,1)S(1)}, u32[]{:S(2)}, u32[]{:S(2)}) async-start(bf16[1,4,8,16,128]{4,3,1,0,2:T(8,128)(2,1)} %copy.40), calls=%async_computation.3 | async-start | bytes 262144 | tf_op jit(solution)/shard_map/all_to_all | solution.py:106
  41.7 0.1 collective-permute-done.2
  41.8 0.0 copy-done
  41.8 0.4 bitcast_reduce_fusion
  42.3 0.4 fusion.1
  42.7 0.5 %divide_convert_fusion = bf16[2,256,128]{1,2,0:T(8,128)(2,1)S(1)} fusion(f32[2,256]{1,0:T(2,128)S(1)} %get-tuple-element.11, bf16[2,1024,128]{1,2,0:T(8,128)(2,1)S(1)} %all_gather.3, f32[2,1024,256]{2,1,0:T(8,128)S(1)} %get-tuple-element.15, f32[2,256]{1,0:T(2,128)S(1)} %get-tuple-element.14, f32[2,256]{1,0:T(2,128)S(1)} %get-tuple-element.10), kind=kOutput, calls=%fused_computation.13 | convolution fusion | flops 135987200 | bytes 2758656 | tf_op jit(solution)/shard_map/frn,fnd->frd/dot_general | solution.py:32
  43.2 5.2 %all-to-all-done.3 = bf16[1,4,8,16,128]{4,3,1,0,2:T(8,128)(2,1)S(1)} async-done(((bf16[1,4,8,16,128]{4,3,1,0,2:T(8,128)(2,1)}), bf16[1,4,8,16,128]{4,3,1,0,2:T(8,128)(2,1)S(1)}, u32[]{:S(2)}, u32[]{:S(2)}) %all-to-all-start.3) | async-done | bytes 131104 | tf_op jit(solution)/shard_map/all_to_all | solution.py:106
  48.4 0.1 copy.43
  48.5 0.8 %copy.44 = bf16[2,256,256]{2,1,0:T(8,128)(2,1)} copy(bf16[2,256,256]{1,2,0:T(8,128)(2,1)S(1)} %pad_maximum_fusion) | data formatting | bytes 524288 | tf_op jit(solution)/shard_map/concatenate | solution.py:118
  (10 shorter events, 0.2 us)
Async XLA Ops:
  0.0 9.8 %copy-start.1 = (bf16[2,256,256]{2,1,0:T(8,128)(2,1)S(1)}, bf16[2,256,256]{2,1,0:T(8,128)(2,1)}, u32[]{:S(2)}) copy-start(bf16[2,256,256]{2,1,0:T(8,128)(2,1)} %param.5) | copy-start | bytes 786436
  1.6 12.4 %all-to-all-start = ((bf16[4,4,2,16,128]{4,3,2,1,0:T(8,128)(2,1)}), bf16[4,4,2,16,128]{4,3,2,1,0:T(8,128)(2,1)S(1)}, u32[]{:S(2)}, u32[]{:S(2)}) async-start(bf16[4,4,2,16,128]{4,3,2,1,0:T(8,128)(2,1)} %copy.33), calls=%async_computation | async-start | bytes 262144 | tf_op jit(solution)/shard_map/all_to_all | solution.py:80
  9.1 16.1 %collective-permute-start = (bf16[2,256,128]{2,1,0:T(8,128)(2,1)S(1)}, bf16[2,256,128]{2,1,0:T(8,128)(2,1)S(1)}, u32[]{:S(2)}, u32[]{:S(2)}) collective-permute-start(bf16[2,256,128]{2,1,0:T(8,128)(2,1)S(1)} %get-tuple-element.7), channel_id=1, source_target_pairs={{0,1},{1,2},{2,3},{3,0},{4,5},{5,6},{6,7},{7,4},{8,9},{9,10},{10,1... | collective-permute-start | bytes 393224 | tf_op jit(solution)/shard_map/ppermute | solution.py:17
  14.0 11.6 %all-to-all-start.1 = ((bf16[4,4,2,16,128]{4,3,2,1,0:T(8,128)(2,1)}), bf16[4,4,2,16,128]{4,3,2,1,0:T(8,128)(2,1)S(1)}, u32[]{:S(2)}, u32[]{:S(2)}) async-start(bf16[4,4,2,16,128]{4,3,2,1,0:T(8,128)(2,1)} %copy.35), calls=%async_computation.1 | async-start | bytes 262144 | tf_op jit(solution)/shard_map/all_to_all | solution.py:83
  25.2 12.1 %collective-permute-start.1 = (bf16[2,256,128]{2,1,0:T(8,128)(2,1)S(1)}, bf16[2,256,128]{2,1,0:T(8,128)(2,1)S(1)}, u32[]{:S(2)}, u32[]{:S(2)}) collective-permute-start(bf16[2,256,128]{2,1,0:T(8,128)(2,1)S(1)} %collective-permute-done), channel_id=1, source_target_pairs={{0,1},{1,2},{2,3},{3,0},{4,5},{5,6},{6,7},{7,4},{8,9},{9,10},{10,1... | collective-permute-start | bytes 393224 | tf_op jit(solution)/shard_map/ppermute | solution.py:17
  25.6 16.3 %copy-start = (bf16[2,256,256]{2,1,0:T(8,128)(2,1)S(1)}, bf16[2,256,256]{2,1,0:T(8,128)(2,1)}, u32[]{:S(2)}) copy-start(bf16[2,256,256]{2,1,0:T(8,128)(2,1)} %param.3) | copy-start | bytes 786436
  25.6 11.7 %all-to-all-start.2 = ((bf16[4,4,2,16,128]{4,3,2,1,0:T(8,128)(2,1)}), bf16[4,4,2,16,128]{4,3,2,1,0:T(8,128)(2,1)S(1)}, u32[]{:S(2)}, u32[]{:S(2)}) async-start(bf16[4,4,2,16,128]{4,3,2,1,0:T(8,128)(2,1)} %copy.37), calls=%async_computation.2 | async-start | bytes 262144 | tf_op jit(solution)/shard_map/all_to_all | solution.py:84
  37.4 4.4 %collective-permute-start.2 = (bf16[2,256,128]{2,1,0:T(8,128)(2,1)S(1)}, bf16[2,256,128]{2,1,0:T(8,128)(2,1)S(1)}, u32[]{:S(2)}, u32[]{:S(2)}) collective-permute-start(bf16[2,256,128]{2,1,0:T(8,128)(2,1)S(1)} %collective-permute-done.1), channel_id=1, source_target_pairs={{0,1},{1,2},{2,3},{3,0},{4,5},{5,6},{6,7},{7,4},{8,9},{9,10},{10,1... | collective-permute-start | bytes 393224 | tf_op jit(solution)/shard_map/ppermute | solution.py:17
  38.3 10.0 %all-to-all-start.3 = ((bf16[1,4,8,16,128]{4,3,1,0,2:T(8,128)(2,1)}), bf16[1,4,8,16,128]{4,3,1,0,2:T(8,128)(2,1)S(1)}, u32[]{:S(2)}, u32[]{:S(2)}) async-start(bf16[1,4,8,16,128]{4,3,1,0,2:T(8,128)(2,1)} %copy.40), calls=%async_computation.3 | async-start | bytes 262144 | tf_op jit(solution)/shard_map/all_to_all | solution.py:106
